TPU v7x, 128 devices: a whole 4x4x4 slice. The times are simulated.
128 devices in a mesh: dom: 64 (over x, z, y), batch: 2 (over core).
Axes of the slice: x: 4, y: 4, z: 4, core: 2. Of those that a mesh axis runs over, the one named last changes fastest.
Arguments:
- features: bfloat16 [4, 65536, 512], P('batch', 'dom'), may hold values from -6 to 6
- tile_vals: bfloat16 [2048, 128, 128], P('dom'), may hold values from -0.25 to 0.25
- tile_row: int32 [2048], P('dom'), may hold values from 0 to 7
- tile_col: int32 [2048], P('dom'), may hold values from 0 to 11
- send_next: int32 [128], P('dom'), may hold values from 0 to 7
- send_prev: int32 [128], P('dom'), may hold values from 0 to 7
- cluster: int32 [65536], P('dom'), may hold values from 0 to 1023, as said below
- cotangent: bfloat16 [4, 65536, 512], P('batch', 'dom'), may hold values from -6 to 6
- self_weight: bfloat16 [512, 512], replicated, may hold values from -0.25 to 0.25
- neighbour_weight: bfloat16 [512, 512], replicated, may hold values from -0.25 to 0.25
- w_coarse: bfloat16 [512, 512], replicated, may hold values from -0.25 to 0.25
Outputs:
- output: bfloat16 [4, 65536, 512], P('batch', 'dom')
- self_weight_gradient: float32 [512, 512], replicated
- neighbour_weight_gradient: float32 [512, 512], replicated
- grad_coarse: float32 [512, 512], replicated
Inputs may be any that keep to these rules, and one draw needn't show every extreme that they name: Within each pair of partitions 2m, 2m + 1, every cluster number names exactly two of the pair's 2 * 1024 nodes.
All inputs are finite; a program needn't handle non-finite values.
Results may differ from a plain program's by a relative error of at most 0.012.
Values may be sent and summed in bfloat16 or wider, within the bound.
A program may use at most 128 MiB of HBM per device.

v0:
```python
import math
import jax
import jax.numpy as jnp
from jax import lax
from jax.sharding import PartitionSpec as P


def shifted(x, axis, by):
    length = lax.axis_size(axis)
    pairs = [(i, i + by) for i in range(length) if 0 <= i + by < length]
    return lax.ppermute(x, axis, pairs)


def partner(value, axis, distance):
    mask = 2**distance
    pairs = [(source, source ^ mask) for source in range(lax.axis_size(axis))]
    return lax.ppermute(value, axis, pairs)


def dsilu(value):
    sig = jax.nn.sigmoid(value)
    return sig * (1.0 + value * (1.0 - sig))


def member_table(labels, count):
    return (labels[None, :] == jnp.arange(count, dtype=jnp.int32)[:, None]).astype(jnp.bfloat16)


def pooling(rows, table):
    return jnp.einsum("cn,snd->scd", table, rows, preferred_element_type=jnp.float32)


def lookup(coarse_rows, table):
    return jnp.einsum("cn,scd->snd", table, coarse_rows, preferred_element_type=jnp.float32)


def pick_blocks(labels, count, tiled):
    table = (labels[:, None] == jnp.arange(count, dtype=jnp.int32)[None, :]).astype(jnp.bfloat16)
    return jnp.einsum("tb,sbjd->stjd", table, tiled, preferred_element_type=jnp.float32).astype(
        jnp.bfloat16
    )


def local(
    features,
    tile_vals,
    tile_row,
    tile_col,
    send_next,
    send_prev,
    cluster,
    cotangent,
    self_weight,
    neighbour_weight,
    w_coarse,
):
    scen, nodes, width = features.shape
    side = tile_vals.shape[1]
    blocks = nodes // side
    tiled = features.reshape(scen, blocks, side, width)
    to_next = pick_blocks(send_next, blocks, tiled)
    to_prev = pick_blocks(send_prev, blocks, tiled)
    got_prev = shifted(to_next, "dom", 1)
    got_next = shifted(to_prev, "dom", -1)
    extended = jnp.concatenate([tiled, got_prev, got_next], axis=1)
    picked = pick_blocks(tile_col, extended.shape[1], extended)
    terms = jnp.einsum("tij,stjd->stid", tile_vals, picked, preferred_element_type=jnp.float32)
    rowhot = (tile_row[None, :] == jnp.arange(blocks, dtype=jnp.int32)[:, None]).astype(jnp.float32)
    summed = jnp.einsum("rt,stid->srid", rowhot, terms, precision=lax.Precision.HIGHEST)
    neighbour_total = summed.reshape(scen, nodes, width).astype(jnp.bfloat16)
    preactivation = jnp.einsum(
        "jkb,bt->jkt", features, self_weight, preferred_element_type=jnp.float32
    )
    preactivation = preactivation + jnp.einsum(
        "jkb,bt->jkt", neighbour_total, neighbour_weight, preferred_element_type=jnp.float32
    )
    hidden = jax.nn.silu(preactivation).astype(jnp.bfloat16)
    table = member_table(cluster, nodes)
    parity = lax.axis_index("dom") % 2
    half = nodes // 2
    own_start = parity * half

    def owned(array):
        return lax.dynamic_slice_in_dim(array, own_start, half, 1)

    partial_value = pooling(hidden, table)
    grad_partial = pooling(cotangent, table)
    partner_sums = partner(partial_value.astype(jnp.bfloat16), "dom", 0).astype(partial_value.dtype)
    coarse = (0.5 * (partial_value + partner_sums)).astype(jnp.bfloat16)
    act = jnp.einsum("skd,de->ske", coarse, w_coarse, preferred_element_type=jnp.float32)
    lifted = jax.nn.silu(act).astype(jnp.bfloat16)
    grad_lift = grad_partial + partner(grad_partial.astype(jnp.bfloat16), "dom", 0).astype(
        grad_partial.dtype
    )
    grad_act = (grad_lift * dsilu(act)).astype(jnp.bfloat16)
    term_coarse = jnp.einsum(
        "skd,ske->de", owned(coarse), owned(grad_act), preferred_element_type=jnp.float32
    )
    grad_down = jnp.einsum(
        "ske,de->skd", grad_act, w_coarse, preferred_element_type=jnp.float32
    ).astype(jnp.bfloat16)
    spread = lookup(lifted, table)
    output = (hidden.astype(jnp.float32) + spread).astype(jnp.bfloat16)
    back = lookup(grad_down, table)
    grad_hidden = cotangent.astype(jnp.float32) + 0.5 * back
    preactivation_gradient = (grad_hidden * dsilu(preactivation)).astype(jnp.bfloat16)
    self_contribution = jnp.einsum(
        "btv,btq->vq", features, preactivation_gradient, preferred_element_type=jnp.float32
    )
    neighbour_contribution = jnp.einsum(
        "btv,btq->vq", neighbour_total, preactivation_gradient, preferred_element_type=jnp.float32
    )
    totals = lax.psum((self_contribution, neighbour_contribution, term_coarse), ("dom", "batch"))
    gradient_scale = 1.0 / math.sqrt(scen * lax.axis_size("batch") * nodes * lax.axis_size("dom"))
    return (
        output,
        totals[0] * gradient_scale,
        totals[1] * gradient_scale,
        totals[2] * gradient_scale,
    )


def solution(mesh):
    in_specs = (
        P("batch", "dom", None),
        P("dom", None, None),
        P("dom"),
        P("dom"),
        P("dom"),
        P("dom"),
        P("dom"),
        P("batch", "dom", None),
        P(),
        P(),
        P(),
    )
    out_specs = (P("batch", "dom", None), P(), P(), P())
    return jax.shard_map(local, mesh=mesh, in_specs=in_specs, out_specs=out_specs, check_vma=False)
```

profile of v0, /device:TPU:1, one launch (start us, length us, event | category | flops | bytes accessed | tf_op | source)
XLA Modules:
  0.0 384.3 jit_solution(13734323582045857980)
XLA Ops:
  7.2 0.0 copy-start
  7.2 0.0 copy-start.2
  7.2 0.0 all-reduce.3.cloned.1.call-start
  7.2 0.0 copy-start.9
  7.2 3.2 fusion.35
  10.5 4.1 %collective-permute-start = (bf16[2,2,128,512]{3,1,2,0:T(2,128)(2,1)S(1)}, bf16[2,2,128,512]{3,1,2,0:T(2,128)(2,1)S(1)}, u32[]{:S(2)}, u32[]{:S(2)}) collective-permute-start(bf16[2,2,128,512]{3,1,2,0:T(2,128)(2,1)S(1)} %fusion.35), channel_id=1, source_target_pairs={{0,2},{2,4},{4,6},{6,8},{8,10},{10,12},{12,14},{14,16},{16,18},{18... | collective-permute-start | bytes 1572872 | tf_op jit(solution)/shard_map/ppermute | solution.py:11
  14.5 3.1 fusion.36
  17.6 1.3 collective-permute-start.1
  18.9 0.0 copy-done.2
  18.9 1.2 copy.58
  20.1 0.0 copy-done.9
  20.1 0.0 copy-start.15
  20.1 3.3 fusion.45
  23.4 1.7 collective-permute-done
  25.1 6.9 %collective-permute-done.1 = bf16[2,2,128,512]{3,1,2,0:T(2,128)(2,1)S(1)} collective-permute-done((bf16[2,2,128,512]{3,1,2,0:T(2,128)(2,1)S(1)}, bf16[2,2,128,512]{3,1,2,0:T(2,128)(2,1)S(1)}, u32[]{:S(2)}, u32[]{:S(2)}) %collective-permute-start.1) | collective-permute-done | bytes 524320 | tf_op jit(solution)/shard_map/ppermute | solution.py:11
  32.0 5.3 %convert_bitcast_fusion = bf16[2,32,128,512]{3,1,2,0:T(8,128)(2,1)} fusion(bf16[2,2,128,512]{3,1,2,0:T(2,128)(2,1)S(1)} %collective-permute-done.1, bf16[2,2,128,512]{3,1,2,0:T(2,128)(2,1)S(1)} %collective-permute-done, bf16[2,8,128,512]{3,1,2,0:T(8,128)(2,1)S(1)} %copy.58, s32[32]{0:T(128)S(1)} %copy-done.15), kind=kOutput, calls=%fused_computation.2 | convolution fusion | flops 114295168 | bytes 11534464 | tf_op jit(solution)/shard_map/tb,sbjd->stjd/dot_general | solution.py:39
  37.3 18.5 %convolution_bitcast_fusion = f32[2,32,128,512]{2,3,0,1:T(8,128)} fusion(bf16[2,32,128,512]{3,1,2,0:T(8,128)(2,1)} %convert_bitcast_fusion, bf16[32,128,128]{2,1,0:T(8,128)(2,1)S(1)} %copy-done), kind=kOutput, calls=%fused_computation | convolution fusion | flops 1073741824 | bytes 26214400 | tf_op jit(solution)/shard_map/tij,stjd->stid/dot_general | solution.py:67
  55.8 20.1 %copy.60 = f32[2,32,128,512]{3,1,2,0:T(8,128)} copy(f32[2,32,128,512]{2,3,0,1:T(8,128)} %convolution_bitcast_fusion) | data formatting | bytes 33554432 | tf_op jit(solution)/shard_map/tij,stjd->stid/transpose | solution.py:67
  75.8 0.0 copy-done.11
  75.9 9.2 %convert_bitcast_fusion.1 = bf16[2,8,128,512]{3,1,2,0:T(8,128)(2,1)S(1)} fusion(f32[2,32,128,512]{3,1,2,0:T(8,128)} %copy.60, s32[32]{0:T(128)S(1)} %copy-done.11), kind=kOutput, calls=%fused_computation.37 | convolution fusion | flops 403702016 | bytes 18874496 | tf_op jit(solution)/shard_map/rt,stid->srid/dot_general | solution.py:69
  85.1 0.0 copy-start.3
  85.1 0.7 copy.61
  85.8 1.3 copy-done.4
  87.1 0.9 copy-done.3
  88.1 1.2 convolution_add_fusion
  89.3 0.0 copy-start.12
  89.3 5.5 %bitcast_convert_fusion.1 = (bf16[2,1024,512]{1,2,0:T(8,128)(2,1)}, f32[2,512,1024]{2,1,0:T(8,128)}) fusion(s32[1024]{0:T(1024)S(1)} %copy-done.14, f32[2,1024,512]{2,1,0:T(8,128)S(1)} %convolution_add_fusion), kind=kOutput, calls=%fused_computation.18 | convolution fusion | flops 2154823680 | bytes 10489856 | tf_op jit(solution)/shard_map/cn,snd->scd/dot_general | solution.py:30
  94.8 1.3 collective-permute-start.2
  96.1 5.0 %bitcast_convert_fusion = (bf16[2,1024,512]{2,1,0:T(8,128)(2,1)}, f32[1024,2,512]{2,0,1:T(8,128)}) fusion(bf16[2,1024,512]{2,1,0:T(8,128)(2,1)S(1)} %copy-done.12, s32[1024]{0:T(1024)S(1)} %copy-done.14), kind=kOutput, calls=%fused_computation.12 | convolution fusion | flops 2149580800 | bytes 8392704 | tf_op jit(solution)/shard_map/cn,snd->scd/dot_general | solution.py:30
  101.1 0.4 collective-permute-start.3
  101.5 38.9 %collective-permute-done.2 = bf16[2,1024,512]{1,2,0:T(8,128)(2,1)} collective-permute-done((bf16[2,1024,512]{1,2,0:T(8,128)(2,1)}, bf16[2,1024,512]{1,2,0:T(8,128)(2,1)}, u32[]{:S(2)}, u32[]{:S(2)}) %collective-permute-start.2) | collective-permute-done | bytes 2097184 | tf_op jit(solution)/shard_map/ppermute | solution.py:17
  140.4 3.8 fusion.12
  144.2 41.1 %collective-permute-done.3 = bf16[2,1024,512]{2,1,0:T(8,128)(2,1)} collective-permute-done((bf16[2,1024,512]{2,1,0:T(8,128)(2,1)}, bf16[2,1024,512]{2,1,0:T(8,128)(2,1)}, u32[]{:S(2)}, u32[]{:S(2)}) %collective-permute-start.3) | collective-permute-done | bytes 2097184 | tf_op jit(solution)/shard_map/ppermute | solution.py:17
  185.3 0.0 copy-done.13
  185.3 6.8 %fusion.9 = (bf16[2,1024,512]{2,1,0:T(8,128)(2,1)}, f32[2,1024,512]{2,1,0:T(8,128)}) fusion(f32[1024,2,512]{2,0,1:T(8,128)S(1)} %copy-done.17, bf16[2,1024,512]{2,1,0:T(8,128)(2,1)} %collective-permute-done.3, bf16[2,1024,512]{1,2,0:T(8,128)(2,1)S(1)} %fusion.12, bf16[512,512]{1,0:T(8,128)(2,1)S(1)} %copy-done.13), kind=kOutput, calls=%fused_computation.14 | convolution fusion | flops 1085276160 | bytes 15204352 | tf_op jit(solution)/shard_map/skd,de->ske/dot_general | solution.py:90
  192.1 8.1 %fusion.7 = bf16[2,1024,512]{2,1,0:T(8,128)(2,1)} fusion(f32[2,1024,512]{2,1,0:T(8,128)} %copy-done.5, bf16[2,1024,512]{2,1,0:T(8,128)(2,1)} %param.18, s32[1024]{0:T(1024)S(1)} %copy-done.14, bf16[2,1024,512]{2,1,0:T(8,128)(2,1)} %get-tuple-element.27, bf16[512,512]{1,0:T(8,128)(2,1)S(1)} %copy-done.13), kind=kOutput, calls=%fused_computation.10 | convolution fusion | flops 3235905536 | bytes 11014144 | tf_op jit(solution)/shard_map/cn,scd->snd/dot_general | solution.py:34
  200.2 4.6 %convolution_bitcast_fusion.2 = f32[512,512]{0,1:T(8,128)} fusion(bf16[2,1024,512]{2,1,0:T(8,128)(2,1)} %bitcast.111, bf16[2,1024,512]{2,1,0:T(8,128)(2,1)} %fusion.7), kind=kOutput, calls=%fused_computation.40 | convolution fusion | flops 1073741824 | bytes 5242880 | tf_op jit(solution)/shard_map/btv,btq->vq/dot_general | solution.py:110
  204.8 2.2 convolution_bitcast_fusion.3
  207.0 1.7 convolution_bitcast_fusion.1
  208.8 0.0 all-reduce.3.cloned.1.call-update
  208.8 8.0 %fusion.10 = bf16[2,1024,512]{2,1,0:T(8,128)(2,1)} fusion(s32[1024]{0:T(1024)S(1)} %copy-done.14, f32[2,1024,512]{2,1,0:T(8,128)} %get-tuple-element.28, f32[2,1024,512]{2,1,0:T(8,128)} %copy-done.5), kind=kOutput, calls=%fused_computation.16 | convolution fusion | flops 2162163712 | bytes 10489856 | tf_op jit(solution)/shard_map/cn,scd->snd/dot_general | solution.py:34
  216.8 153.4 %all-reduce.3.cloned.1.call-done = (f32[512,512]{0,1:T(8,128)}, f32[512,512]{0,1:T(8,128)}, f32[512,512]{0,1:T(8,128)}) async-done(((f32[512,512]{0,1:T(8,128)}, f32[512,512]{0,1:T(8,128)}, f32[512,512]{0,1:T(8,128)}), (f32[512,512]{0,1:T(8,128)}, f32[512,512]{0,1:T(8,128)}, f32[512,512]{0,1:T(8,128)})) %all-reduce.3.cloned.1.call-update) | async-done | bytes 3145744 | tf_op jit(solution)/shard_map/psum | solution.py:113
  370.2 1.8 broadcast_multiply_fusion
  371.9 0.0 copy-start.1
  372.0 1.3 copy.73
  373.3 1.3 copy.74
  374.6 1.3 broadcast_multiply_fusion.2
  375.9 1.3 copy.72
  (23 shorter events, 0.0 us)
Async XLA Ops:
  7.2 30.1 %copy-start = (bf16[32,128,128]{2,1,0:T(8,128)(2,1)S(1)}, bf16[32,128,128]{2,1,0:T(8,128)(2,1)}, u32[]{:S(2)}) copy-start(bf16[32,128,128]{2,1,0:T(8,128)(2,1)} %param.12) | copy-start | bytes 3145732
  7.2 11.7 %copy-start.2 = (bf16[2,1024,512]{2,1,0:T(8,128)(2,1)S(1)}, bf16[2,1024,512]{2,1,0:T(8,128)(2,1)}, u32[]{:S(2)}) copy-start(bf16[2,1024,512]{2,1,0:T(8,128)(2,1)} %param.11) | copy-start | bytes 6291460
  7.2 363.0 %all-reduce.3.cloned.1.call-start = ((), (), s32[]{:S(2)}) async-start(), calls=%async_computation | async-start | bytes 6291456 | tf_op jit(solution)/shard_map/psum | solution.py:113
  7.2 12.8 %copy-start.9 = (bf16[512,512]{1,0:T(8,128)(2,1)S(1)}, bf16[512,512]{1,0:T(8,128)(2,1)}, u32[]{:S(2)}) copy-start(bf16[512,512]{1,0:T(8,128)(2,1)} %param.19) | copy-start | bytes 1572868
  10.5 14.6 %collective-permute-start = (bf16[2,2,128,512]{3,1,2,0:T(2,128)(2,1)S(1)}, bf16[2,2,128,512]{3,1,2,0:T(2,128)(2,1)S(1)}, u32[]{:S(2)}, u32[]{:S(2)}) collective-permute-start(bf16[2,2,128,512]{3,1,2,0:T(2,128)(2,1)S(1)} %fusion.35), channel_id=1, source_target_pairs={{0,2},{2,4},{4,6},{6,8},{8,10},{10,12},{12,14},{14,16},{16,18},{18... | collective-permute-start | bytes 1572872 | tf_op jit(solution)/shard_map/ppermute | solution.py:11
  17.6 14.4 %collective-permute-start.1 = (bf16[2,2,128,512]{3,1,2,0:T(2,128)(2,1)S(1)}, bf16[2,2,128,512]{3,1,2,0:T(2,128)(2,1)S(1)}, u32[]{:S(2)}, u32[]{:S(2)}) collective-permute-start(bf16[2,2,128,512]{3,1,2,0:T(2,128)(2,1)S(1)} %fusion.36), channel_id=1, source_target_pairs={{2,0},{4,2},{6,4},{8,6},{10,8},{12,10},{14,12},{16,14},{18,16},{20... | collective-permute-start | bytes 1572872 | tf_op jit(solution)/shard_map/ppermute | solution.py:11
  20.1 11.9 %copy-start.15 = (s32[32]{0:T(128)S(1)}, s32[32]{0:T(128)}, u32[]{:S(2)}) copy-start(s32[32]{0:T(128)} %param.14) | copy-start | bytes 388
  55.8 20.1 %copy-start.11 = (s32[32]{0:T(128)S(1)}, s32[32]{0:T(128)}, u32[]{:S(2)}) copy-start(s32[32]{0:T(128)} %param.13) | copy-start | bytes 388
  75.8 11.3 %copy-start.10 = (bf16[512,512]{1,0:T(8,128)(2,1)S(1)}, bf16[512,512]{1,0:T(8,128)(2,1)}, u32[]{:S(2)}) copy-start(bf16[512,512]{1,0:T(8,128)(2,1)} %param.20) | copy-start | bytes 1572868
  85.1 2.9 copy-start.3
  85.8 1.3 copy-start.4
  88.1 1.3 copy-start.14
  89.3 5.5 %copy-start.5 = (f32[2,1024,512]{2,1,0:T(8,128)}, f32[2,1024,512]{2,1,0:T(8,128)S(1)}, u32[]{:S(2)}) copy-start(f32[2,1024,512]{2,1,0:T(8,128)S(1)} %convolution_add_fusion) | copy-start | bytes 12582916
  89.3 6.8 %copy-start.12 = (bf16[2,1024,512]{2,1,0:T(8,128)(2,1)S(1)}, bf16[2,1024,512]{2,1,0:T(8,128)(2,1)}, u32[]{:S(2)}) copy-start(bf16[2,1024,512]{2,1,0:T(8,128)(2,1)} %param.18) | copy-start | bytes 6291460
  94.8 45.6 %collective-permute-start.2 = (bf16[2,1024,512]{1,2,0:T(8,128)(2,1)}, bf16[2,1024,512]{1,2,0:T(8,128)(2,1)}, u32[]{:S(2)}, u32[]{:S(2)}) collective-permute-start(bf16[2,1024,512]{1,2,0:T(8,128)(2,1)} %get-tuple-element.23), channel_id=1, source_target_pairs={{0,2},{2,0},{4,6},{6,4},{8,10},{10,8},{12,14},{14,12},{16,18},{18,... | collective-permute-start | bytes 6291464 | tf_op jit(solution)/shard_map/ppermute | solution.py:17
  101.1 84.2 %collective-permute-start.3 = (bf16[2,1024,512]{2,1,0:T(8,128)(2,1)}, bf16[2,1024,512]{2,1,0:T(8,128)(2,1)}, u32[]{:S(2)}, u32[]{:S(2)}) collective-permute-start(bf16[2,1024,512]{2,1,0:T(8,128)(2,1)} %get-tuple-element.25), channel_id=1, source_target_pairs={{0,2},{2,0},{4,6},{6,4},{8,10},{10,8},{12,14},{14,12},{16,18},{18,... | collective-permute-start | bytes 6291464 | tf_op jit(solution)/shard_map/ppermute | solution.py:17
  140.4 44.9 %copy-start.13 = (bf16[512,512]{1,0:T(8,128)(2,1)S(1)}, bf16[512,512]{1,0:T(8,128)(2,1)}, u32[]{:S(2)}) copy-start(bf16[512,512]{1,0:T(8,128)(2,1)} %param.21) | copy-start | bytes 1572868
  140.4 44.9 %copy-start.17 = (f32[1024,2,512]{2,0,1:T(8,128)S(1)}, f32[1024,2,512]{2,0,1:T(8,128)}, u32[]{:S(2)}) copy-start(f32[1024,2,512]{2,0,1:T(8,128)} %get-tuple-element.26) | copy-start | bytes 12582916
  144.2 47.9 %copy-start.7 = (bf16[2,1024,512]{1,2,0:T(8,128)(2,1)}, bf16[2,1024,512]{1,2,0:T(8,128)(2,1)S(1)}, u32[]{:S(2)}) copy-start(bf16[2,1024,512]{1,2,0:T(8,128)(2,1)S(1)} %fusion.12) | copy-start | bytes 6291460
  200.2 4.6 %copy-start.6 = (bf16[2,1024,512]{2,1,0:T(8,128)(2,1)S(1)}, bf16[2,1024,512]{2,1,0:T(8,128)(2,1)}, u32[]{:S(2)}) copy-start(bf16[2,1024,512]{2,1,0:T(8,128)(2,1)} %fusion.7) | copy-start | bytes 6291460
  204.8 2.2 copy-start.8
  204.8 2.2 copy-start.16
  371.9 5.3 %copy-start.1 = (bf16[32,128,128]{2,1,0:T(8,128)(2,1)S(1)}, bf16[32,128,128]{2,1,0:T(8,128)(2,1)}, u32[]{:S(2)}) copy-start(bf16[32,128,128]{2,1,0:T(8,128)(2,1)} %param.12) | copy-start | bytes 3145732
Sparse Core Ops, SparseCore 0:
  208.9 161.1 all-reduce.2
where the time goes:
time: 389 us; the launch traced here: 384 us
  waiting for transfers between devices  242 us (62%)
  matrix products  85.8 us (22%)
  local copies, waits for them, and re-layouts  28.1 us (7%)
  between operations  14.5 us (4%)
  starting transfers between devices  7.05 us (2%)
  other arithmetic  6.86 us (2%)
    psum x1, waiting for transfers between devices, local(): lax.psum((self_contribution, neighbour_contribution, term_coarse), ('dom'...  153 us
    ppermute x2, waiting for transfers between devices, partner(): return lax.ppermute(value, axis, pairs)  80 us
    transpose x1, local copies, waits for them, and re-layouts, local(): jnp.einsum('tij,stjd->stid', tile_vals, picked, preferred_element_type=jn...  20.1 us
    dot_general x1, matrix products, local(): jnp.einsum('tij,stjd->stid', tile_vals, picked, preferred_element_type=jn...  18.5 us
    dot_general x2, matrix products, lookup(): jnp.einsum('cn,scd->snd', table, coarse_rows, preferred_element_type=jnp....  16.1 us
    dot_general x3, matrix products, pick_blocks(): jnp.einsum('tb,sbjd->stjd', table, tiled, preferred_element_type=jnp.floa...  11.6 us
    dot_general x2, matrix products, pooling(): jnp.einsum('cn,snd->scd', table, rows, preferred_element_type=jnp.float32)  10.5 us
    dot_general x1, matrix products, local(): jnp.einsum('rt,stid->srid', rowhot, terms, precision=lax.Precision.HIGHEST)  9.25 us
  transfers between devices with their start and end apart: 5, of which 5 were waited for; matrix products, arithmetic and copies ran while one was open for 6% of the time, Pallas kernels for 0%

commit v1 on v0

--- a/solution.py
+++ b/solution.py
@@ -110,7 +110,9 @@
     neighbour_contribution = jnp.einsum(
         "btv,btq->vq", neighbour_total, preactivation_gradient, preferred_element_type=jnp.float32
     )
-    totals = lax.psum((self_contribution, neighbour_contribution, term_coarse), ("dom", "batch"))
+    totals = lax.psum(
+        lax.psum((self_contribution, neighbour_contribution, term_coarse), "dom"), "batch"
+    )
     gradient_scale = 1.0 / math.sqrt(scen * lax.axis_size("batch") * nodes * lax.axis_size("dom"))
     return (
         output,

time: 389 us -> 402 us (1.033)
  waiting for transfers between devices: 242 us -> 255 us
    psum x1 -> x2, waiting for transfers between devices: 153 us -> 166 us  [the longest x1 142 us: local(): lax.psum((self_contribution, neighbour_contribution, term_coarse), 'dom')]
  transfers between devices with their start and end apart: 5 -> 6, of which waited for: 5 -> 6; matrix products, arithmetic and copies ran while one was open for 6% -> 6% of each run, Pallas kernels for 0% -> 0%
where the time goes in v1:
time: 402 us; the launch traced here: 397 us
  waiting for transfers between devices  255 us (63%)
  matrix products  86 us (21%)
  local copies, waits for them, and re-layouts  28.1 us (7%)
  between operations  14.5 us (4%)
  starting transfers between devices  7.26 us (2%)
  other arithmetic  6.86 us (2%)
    psum x1, waiting for transfers between devices, local(): lax.psum((self_contribution, neighbour_contribution, term_coarse), 'dom')  142 us
    ppermute x2, waiting for transfers between devices, partner(): return lax.ppermute(value, axis, pairs)  80.1 us
    psum x1, waiting for transfers between devices, local(): lax.psum(lax.psum((self_contribution, neighbour_contribution, term_coarse...  23.5 us
    transpose x1, local copies, waits for them, and re-layouts, local(): jnp.einsum('tij,stjd->stid', tile_vals, picked, preferred_element_type=jn...  20 us
    dot_general x1, matrix products, local(): jnp.einsum('tij,stjd->stid', tile_vals, picked, preferred_element_type=jn...  18.5 us
    dot_general x2, matrix products, lookup(): jnp.einsum('cn,scd->snd', table, coarse_rows, preferred_element_type=jnp....  16.1 us
    dot_general x3, matrix products, pick_blocks(): jnp.einsum('tb,sbjd->stjd', table, tiled, preferred_element_type=jnp.floa...  11.4 us
    dot_general x2, matrix products, pooling(): jnp.einsum('cn,snd->scd', table, rows, preferred_element_type=jnp.float32)  10.5 us
  transfers between devices with their start and end apart: 6, of which 6 were waited for; matrix products, arithmetic and copies ran while one was open for 6% of the time, Pallas kernels for 0%

profile of v1, /device:TPU:1, one launch (start us, length us, event | category | flops | bytes accessed | tf_op | source)
XLA Modules:
  0.0 397.2 jit_solution(7552107408937285622)
XLA Ops:
  7.2 0.0 copy-start
  7.2 0.0 copy-start.2
  7.2 0.0 all-reduce.5.cloned.1.call-start
  7.2 3.2 fusion.35
  10.5 4.1 %collective-permute-start = (bf16[2,2,128,512]{3,1,2,0:T(2,128)(2,1)S(1)}, bf16[2,2,128,512]{3,1,2,0:T(2,128)(2,1)S(1)}, u32[]{:S(2)}, u32[]{:S(2)}) collective-permute-start(bf16[2,2,128,512]{3,1,2,0:T(2,128)(2,1)S(1)} %fusion.35), channel_id=1, source_target_pairs={{0,2},{2,4},{4,6},{6,8},{8,10},{10,12},{12,14},{14,16},{16,18},{18... | collective-permute-start | bytes 1572872 | tf_op jit(solution)/shard_map/ppermute | solution.py:11
  14.5 3.1 fusion.36
  17.6 1.3 collective-permute-start.1
  18.9 1.2 copy.58
  20.1 0.0 copy-start.15
  20.1 3.3 fusion.45
  23.4 1.7 collective-permute-done
  25.1 6.9 %collective-permute-done.1 = bf16[2,2,128,512]{3,1,2,0:T(2,128)(2,1)S(1)} collective-permute-done((bf16[2,2,128,512]{3,1,2,0:T(2,128)(2,1)S(1)}, bf16[2,2,128,512]{3,1,2,0:T(2,128)(2,1)S(1)}, u32[]{:S(2)}, u32[]{:S(2)}) %collective-permute-start.1) | collective-permute-done | bytes 524320 | tf_op jit(solution)/shard_map/ppermute | solution.py:11
  32.0 5.1 %convert_bitcast_fusion = bf16[2,32,128,512]{3,1,2,0:T(8,128)(2,1)} fusion(bf16[2,2,128,512]{3,1,2,0:T(2,128)(2,1)S(1)} %collective-permute-done.1, bf16[2,2,128,512]{3,1,2,0:T(2,128)(2,1)S(1)} %collective-permute-done, bf16[2,8,128,512]{3,1,2,0:T(8,128)(2,1)S(1)} %copy.58, s32[32]{0:T(128)S(1)} %copy-done.15), kind=kOutput, calls=%fused_computation.2 | convolution fusion | flops 114295168 | bytes 11534464 | tf_op jit(solution)/shard_map/tb,sbjd->stjd/dot_general | solution.py:39
  37.1 0.0 copy-done
  37.1 18.5 %convolution_bitcast_fusion = f32[2,32,128,512]{2,3,0,1:T(8,128)} fusion(bf16[2,32,128,512]{3,1,2,0:T(8,128)(2,1)} %convert_bitcast_fusion, bf16[32,128,128]{2,1,0:T(8,128)(2,1)S(1)} %copy-done), kind=kOutput, calls=%fused_computation | convolution fusion | flops 1073741824 | bytes 26214400 | tf_op jit(solution)/shard_map/tij,stjd->stid/dot_general | solution.py:67
  55.6 20.0 %copy.60 = f32[2,32,128,512]{3,1,2,0:T(8,128)} copy(f32[2,32,128,512]{2,3,0,1:T(8,128)} %convolution_bitcast_fusion) | data formatting | bytes 33554432 | tf_op jit(solution)/shard_map/tij,stjd->stid/transpose | solution.py:67
  75.6 9.6 %convert_bitcast_fusion.1 = bf16[2,8,128,512]{3,1,2,0:T(8,128)(2,1)S(1)} fusion(f32[2,32,128,512]{3,1,2,0:T(8,128)} %copy.60, s32[32]{0:T(128)S(1)} %copy-done.11), kind=kOutput, calls=%fused_computation.37 | convolution fusion | flops 403702016 | bytes 18874496 | tf_op jit(solution)/shard_map/rt,stid->srid/dot_general | solution.py:69
  85.2 0.7 copy.61
  85.9 0.0 copy-start.4
  85.9 1.3 copy-done.4
  87.2 0.9 copy-done.3
  88.1 1.2 convolution_add_fusion
  89.4 0.0 copy-start.12
  89.4 5.5 %bitcast_convert_fusion.1 = (bf16[2,1024,512]{1,2,0:T(8,128)(2,1)}, f32[2,512,1024]{2,1,0:T(8,128)}) fusion(s32[1024]{0:T(1024)S(1)} %copy-done.14, f32[2,1024,512]{2,1,0:T(8,128)S(1)} %convolution_add_fusion), kind=kOutput, calls=%fused_computation.18 | convolution fusion | flops 2154823680 | bytes 10489856 | tf_op jit(solution)/shard_map/cn,snd->scd/dot_general | solution.py:30
  94.9 1.3 collective-permute-start.2
  96.1 5.0 %bitcast_convert_fusion = (bf16[2,1024,512]{2,1,0:T(8,128)(2,1)}, f32[1024,2,512]{2,0,1:T(8,128)}) fusion(bf16[2,1024,512]{2,1,0:T(8,128)(2,1)S(1)} %copy-done.12, s32[1024]{0:T(1024)S(1)} %copy-done.14), kind=kOutput, calls=%fused_computation.12 | convolution fusion | flops 2149580800 | bytes 8392704 | tf_op jit(solution)/shard_map/cn,snd->scd/dot_general | solution.py:30
  101.2 0.4 collective-permute-start.3
  101.5 38.9 %collective-permute-done.2 = bf16[2,1024,512]{1,2,0:T(8,128)(2,1)} collective-permute-done((bf16[2,1024,512]{1,2,0:T(8,128)(2,1)}, bf16[2,1024,512]{1,2,0:T(8,128)(2,1)}, u32[]{:S(2)}, u32[]{:S(2)}) %collective-permute-start.2) | collective-permute-done | bytes 2097184 | tf_op jit(solution)/shard_map/ppermute | solution.py:17
  140.4 3.8 fusion.12
  144.2 41.1 %collective-permute-done.3 = bf16[2,1024,512]{2,1,0:T(8,128)(2,1)} collective-permute-done((bf16[2,1024,512]{2,1,0:T(8,128)(2,1)}, bf16[2,1024,512]{2,1,0:T(8,128)(2,1)}, u32[]{:S(2)}, u32[]{:S(2)}) %collective-permute-start.3) | collective-permute-done | bytes 2097184 | tf_op jit(solution)/shard_map/ppermute | solution.py:17
  185.4 0.0 copy-done.17
  185.4 6.7 %fusion.9 = (bf16[2,1024,512]{2,1,0:T(8,128)(2,1)}, f32[2,1024,512]{2,1,0:T(8,128)}) fusion(f32[1024,2,512]{2,0,1:T(8,128)S(1)} %copy-done.17, bf16[2,1024,512]{2,1,0:T(8,128)(2,1)} %collective-permute-done.3, bf16[2,1024,512]{1,2,0:T(8,128)(2,1)S(1)} %fusion.12, bf16[512,512]{1,0:T(8,128)(2,1)S(1)} %copy-done.13), kind=kOutput, calls=%fused_computation.14 | convolution fusion | flops 1085276160 | bytes 15204352 | tf_op jit(solution)/shard_map/skd,de->ske/dot_general | solution.py:90
  192.1 8.1 %fusion.7 = bf16[2,1024,512]{2,1,0:T(8,128)(2,1)} fusion(f32[2,1024,512]{2,1,0:T(8,128)} %copy-done.5, bf16[2,1024,512]{2,1,0:T(8,128)(2,1)} %param.18, s32[1024]{0:T(1024)S(1)} %copy-done.14, bf16[2,1024,512]{2,1,0:T(8,128)(2,1)} %get-tuple-element.30, bf16[512,512]{1,0:T(8,128)(2,1)S(1)} %copy-done.13), kind=kOutput, calls=%fused_computation.10 | convolution fusion | flops 3235905536 | bytes 11014144 | tf_op jit(solution)/shard_map/cn,scd->snd/dot_general | solution.py:34
  200.2 4.6 %convolution_bitcast_fusion.2 = f32[512,512]{0,1:T(8,128)} fusion(bf16[2,1024,512]{2,1,0:T(8,128)(2,1)} %bitcast.111, bf16[2,1024,512]{2,1,0:T(8,128)(2,1)} %fusion.7), kind=kOutput, calls=%fused_computation.40 | convolution fusion | flops 1073741824 | bytes 5242880 | tf_op jit(solution)/shard_map/btv,btq->vq/dot_general | solution.py:110
  204.9 2.2 convolution_bitcast_fusion.3
  207.1 1.7 convolution_bitcast_fusion.1
  208.8 0.0 all-reduce.5.cloned.1.call-update
  208.9 0.3 all-reduce.7.cloned.1.call-start
  209.1 142.5 %all-reduce.5.cloned.1.call-done = (f32[512,512]{0,1:T(8,128)}, f32[512,512]{0,1:T(8,128)}, f32[512,512]{0,1:T(8,128)}) async-done(((f32[512,512]{0,1:T(8,128)}, f32[512,512]{0,1:T(8,128)}, f32[512,512]{0,1:T(8,128)}), (f32[512,512]{0,1:T(8,128)}, f32[512,512]{0,1:T(8,128)}, f32[512,512]{0,1:T(8,128)})) %all-reduce.5.cloned.1.call-update) | async-done | bytes 3145744 | tf_op jit(solution)/shard_map/psum | solution.py:114
  351.6 0.0 all-reduce.7.cloned.1.call-update
  351.7 8.0 %fusion.10 = bf16[2,1024,512]{2,1,0:T(8,128)(2,1)} fusion(s32[1024]{0:T(1024)S(1)} %copy-done.14, f32[2,1024,512]{2,1,0:T(8,128)} %get-tuple-element.31, f32[2,1024,512]{2,1,0:T(8,128)} %copy-done.5), kind=kOutput, calls=%fused_computation.16 | convolution fusion | flops 2162163712 | bytes 10489856 | tf_op jit(solution)/shard_map/cn,scd->snd/dot_general | solution.py:34
  359.6 23.5 %all-reduce.7.cloned.1.call-done = (f32[512,512]{0,1:T(8,128)}, f32[512,512]{0,1:T(8,128)}, f32[512,512]{0,1:T(8,128)}) async-done(((f32[512,512]{0,1:T(8,128)}, f32[512,512]{0,1:T(8,128)}, f32[512,512]{0,1:T(8,128)}), (f32[512,512]{0,1:T(8,128)}, f32[512,512]{0,1:T(8,128)}, f32[512,512]{0,1:T(8,128)})) %all-reduce.7.cloned.1.call-update) | async-done | bytes 3145744 | tf_op jit(solution)/shard_map/psum | solution.py:113
  383.1 1.8 broadcast_multiply_fusion
  384.9 0.0 copy-start.1
  384.9 1.3 copy.73
  386.2 1.3 copy.74
  387.5 1.3 broadcast_multiply_fusion.2
  388.9 1.3 copy.72
  (26 shorter events, 0.1 us)
Async XLA Ops:
  7.2 29.9 %copy-start = (bf16[32,128,128]{2,1,0:T(8,128)(2,1)S(1)}, bf16[32,128,128]{2,1,0:T(8,128)(2,1)}, u32[]{:S(2)}) copy-start(bf16[32,128,128]{2,1,0:T(8,128)(2,1)} %param.12) | copy-start | bytes 3145732
  7.2 11.7 %copy-start.2 = (bf16[2,1024,512]{2,1,0:T(8,128)(2,1)S(1)}, bf16[2,1024,512]{2,1,0:T(8,128)(2,1)}, u32[]{:S(2)}) copy-start(bf16[2,1024,512]{2,1,0:T(8,128)(2,1)} %param.11) | copy-start | bytes 6291460
  7.2 344.4 %all-reduce.5.cloned.1.call-start = ((), (), s32[]{:S(2)}) async-start(), calls=%async_computation | async-start | bytes 6291456 | tf_op jit(solution)/shard_map/psum | solution.py:114
  7.2 12.8 %copy-start.9 = (bf16[512,512]{1,0:T(8,128)(2,1)S(1)}, bf16[512,512]{1,0:T(8,128)(2,1)}, u32[]{:S(2)}) copy-start(bf16[512,512]{1,0:T(8,128)(2,1)} %param.19) | copy-start | bytes 1572868
  10.5 14.6 %collective-permute-start = (bf16[2,2,128,512]{3,1,2,0:T(2,128)(2,1)S(1)}, bf16[2,2,128,512]{3,1,2,0:T(2,128)(2,1)S(1)}, u32[]{:S(2)}, u32[]{:S(2)}) collective-permute-start(bf16[2,2,128,512]{3,1,2,0:T(2,128)(2,1)S(1)} %fusion.35), channel_id=1, source_target_pairs={{0,2},{2,4},{4,6},{6,8},{8,10},{10,12},{12,14},{14,16},{16,18},{18... | collective-permute-start | bytes 1572872 | tf_op jit(solution)/shard_map/ppermute | solution.py:11
  17.6 14.4 %collective-permute-start.1 = (bf16[2,2,128,512]{3,1,2,0:T(2,128)(2,1)S(1)}, bf16[2,2,128,512]{3,1,2,0:T(2,128)(2,1)S(1)}, u32[]{:S(2)}, u32[]{:S(2)}) collective-permute-start(bf16[2,2,128,512]{3,1,2,0:T(2,128)(2,1)S(1)} %fusion.36), channel_id=1, source_target_pairs={{2,0},{4,2},{6,4},{8,6},{10,8},{12,10},{14,12},{16,14},{18,16},{20... | collective-permute-start | bytes 1572872 | tf_op jit(solution)/shard_map/ppermute | solution.py:11
  20.1 11.9 %copy-start.15 = (s32[32]{0:T(128)S(1)}, s32[32]{0:T(128)}, u32[]{:S(2)}) copy-start(s32[32]{0:T(128)} %param.14) | copy-start | bytes 388
  55.6 20.0 %copy-start.11 = (s32[32]{0:T(128)S(1)}, s32[32]{0:T(128)}, u32[]{:S(2)}) copy-start(s32[32]{0:T(128)} %param.13) | copy-start | bytes 388
  75.6 11.6 %copy-start.10 = (bf16[512,512]{1,0:T(8,128)(2,1)S(1)}, bf16[512,512]{1,0:T(8,128)(2,1)}, u32[]{:S(2)}) copy-start(bf16[512,512]{1,0:T(8,128)(2,1)} %param.20) | copy-start | bytes 1572868
  85.2 2.9 copy-start.3
  85.9 1.3 copy-start.4
  88.1 1.3 copy-start.14
  89.4 5.5 %copy-start.5 = (f32[2,1024,512]{2,1,0:T(8,128)}, f32[2,1024,512]{2,1,0:T(8,128)S(1)}, u32[]{:S(2)}) copy-start(f32[2,1024,512]{2,1,0:T(8,128)S(1)} %convolution_add_fusion) | copy-start | bytes 12582916
  89.4 6.7 %copy-start.12 = (bf16[2,1024,512]{2,1,0:T(8,128)(2,1)S(1)}, bf16[2,1024,512]{2,1,0:T(8,128)(2,1)}, u32[]{:S(2)}) copy-start(bf16[2,1024,512]{2,1,0:T(8,128)(2,1)} %param.18) | copy-start | bytes 6291460
  94.9 45.6 %collective-permute-start.2 = (bf16[2,1024,512]{1,2,0:T(8,128)(2,1)}, bf16[2,1024,512]{1,2,0:T(8,128)(2,1)}, u32[]{:S(2)}, u32[]{:S(2)}) collective-permute-start(bf16[2,1024,512]{1,2,0:T(8,128)(2,1)} %get-tuple-element.26), channel_id=1, source_target_pairs={{0,2},{2,0},{4,6},{6,4},{8,10},{10,8},{12,14},{14,12},{16,18},{18,... | collective-permute-start | bytes 6291464 | tf_op jit(solution)/shard_map/ppermute | solution.py:17
  101.2 84.2 %collective-permute-start.3 = (bf16[2,1024,512]{2,1,0:T(8,128)(2,1)}, bf16[2,1024,512]{2,1,0:T(8,128)(2,1)}, u32[]{:S(2)}, u32[]{:S(2)}) collective-permute-start(bf16[2,1024,512]{2,1,0:T(8,128)(2,1)} %get-tuple-element.28), channel_id=1, source_target_pairs={{0,2},{2,0},{4,6},{6,4},{8,10},{10,8},{12,14},{14,12},{16,18},{18,... | collective-permute-start | bytes 6291464 | tf_op jit(solution)/shard_map/ppermute | solution.py:17
  140.4 44.9 %copy-start.13 = (bf16[512,512]{1,0:T(8,128)(2,1)S(1)}, bf16[512,512]{1,0:T(8,128)(2,1)}, u32[]{:S(2)}) copy-start(bf16[512,512]{1,0:T(8,128)(2,1)} %param.21) | copy-start | bytes 1572868
  140.4 44.9 %copy-start.17 = (f32[1024,2,512]{2,0,1:T(8,128)S(1)}, f32[1024,2,512]{2,0,1:T(8,128)}, u32[]{:S(2)}) copy-start(f32[1024,2,512]{2,0,1:T(8,128)} %get-tuple-element.29) | copy-start | bytes 12582916
  144.2 47.9 %copy-start.7 = (bf16[2,1024,512]{1,2,0:T(8,128)(2,1)}, bf16[2,1024,512]{1,2,0:T(8,128)(2,1)S(1)}, u32[]{:S(2)}) copy-start(bf16[2,1024,512]{1,2,0:T(8,128)(2,1)S(1)} %fusion.12) | copy-start | bytes 6291460
  200.2 4.6 %copy-start.6 = (bf16[2,1024,512]{2,1,0:T(8,128)(2,1)S(1)}, bf16[2,1024,512]{2,1,0:T(8,128)(2,1)}, u32[]{:S(2)}) copy-start(bf16[2,1024,512]{2,1,0:T(8,128)(2,1)} %fusion.7) | copy-start | bytes 6291460
  204.9 2.3 copy-start.8
  204.9 2.3 copy-start.16
  208.9 174.3 %all-reduce.7.cloned.1.call-start = ((), (), s32[]{:S(2)}) async-start(), calls=%async_computation.1 | async-start | bytes 6291456 | tf_op jit(solution)/shard_map/psum | solution.py:113
  384.9 5.3 %copy-start.1 = (bf16[32,128,128]{2,1,0:T(8,128)(2,1)S(1)}, bf16[32,128,128]{2,1,0:T(8,128)(2,1)}, u32[]{:S(2)}) copy-start(bf16[32,128,128]{2,1,0:T(8,128)(2,1)} %param.12) | copy-start | bytes 3145732
Sparse Core Ops, SparseCore 0:
  209.0 142.5 all-reduce.4
  354.4 28.6 all-reduce.6
